TPU v7x, 256 devices: a whole 4x4x8 slice. The times are simulated.
256 devices in a mesh: expert: 128 (over z, x, y), dp: 2 (over core).
Axes of the slice: x: 4, y: 4, z: 8, core: 2. Of those that a mesh axis runs over, the one named last changes fastest.
Arguments:
- tokens: bfloat16 [32768, 7168], P(('expert', 'dp')), may hold values from -6 to 6
- cotangent: bfloat16 [32768, 7168], P(('expert', 'dp')), may hold values from -6 to 6
- logits: float32 [32768, 256], P(('expert', 'dp')), may hold values from -8 to 8
- expert_ids: int32 [32768, 8], P(('expert', 'dp')), may hold values from 0 to 255, all different within a row; in each aligned block of 128 rows (0 to 127, 128 to 255, ...) at most 5 rows name the same one
- gate_proj: bfloat16 [128, 7168, 128], P('expert'), may hold values from -0.0625 to 0.0625
- up_proj: bfloat16 [128, 7168, 128], P('expert'), may hold values from -0.0625 to 0.0625
- down_proj: bfloat16 [128, 128, 7168], P('expert'), may hold values from -0.125 to 0.125
Outputs:
- token_grad: bfloat16 [32768, 7168], P(('expert', 'dp'))
- logit_grad: float32 [32768, 256], P(('expert', 'dp'))
- down_grad: bfloat16 [128, 128, 7168], P('expert', None, 'dp')
Inputs may be any that keep to these rules, and one draw needn't show every extreme that they name: `expert_ids`: each row names 8 different experts. Within the 128 rows of one device no expert is named more than 5 times, a bound that some block reaches.
All inputs are finite; a program needn't handle non-finite values.
Results may differ from a plain program's by a relative error of at most 0.012.
Values may be sent and summed in bfloat16 or wider, within the bound.
A program may use at most 192 MiB of HBM per device.

v0:
```python
import jax
import jax.numpy as jnp
from jax import lax
from jax.sharding import PartitionSpec as P

SPLIT = 16


SCALE = 2.5


def slot_ranks(block_ids, experts):
    flat = block_ids.reshape(-1)
    onehot = (flat[:, None] == jnp.arange(experts, dtype=jnp.int32)[None, :]).astype(jnp.int32)
    before = jnp.cumsum(onehot, axis=0) - onehot
    return jnp.sum(before * onehot, axis=1)


def router_weights(logits, expert_ids):
    experts = logits.shape[1]
    pick = (expert_ids[:, :, None] == jnp.arange(experts, dtype=jnp.int32)[None, None, :]).astype(
        jnp.float32
    )
    chosen = jnp.sum(pick * jax.nn.sigmoid(logits)[:, None, :], axis=2)
    total = jnp.sum(chosen, axis=1, keepdims=True)
    return (pick, chosen, total, SCALE * chosen / total)


def router_grad(pick, chosen, total, dweight):
    inner = jnp.sum(dweight * chosen, axis=1, keepdims=True) / total
    dchosen = SCALE / total * (dweight - inner)
    dlogit = dchosen * chosen * (1.0 - chosen)
    return jnp.sum(pick * dlogit[:, :, None], axis=1)


def expert_forward(rows, gate, up):
    gated = jnp.dot(rows, gate, preferred_element_type=jnp.float32)
    upped = jnp.dot(rows, up, preferred_element_type=jnp.float32)
    sig = jax.nn.sigmoid(gated)
    active = gated * sig
    hidden = (active * upped).astype(jnp.bfloat16)
    return (gated, upped, sig, active, hidden)


def expert_backward(forward, cot, weight_b, gate, up, down):
    gated, upped, sig, active, hidden = forward
    contract = (((1,), (1,)), ((), ()))
    proj = lax.dot_general(cot, down, contract, preferred_element_type=jnp.float32)
    dots = jnp.sum(hidden.astype(jnp.float32) * proj, axis=1).astype(jnp.bfloat16)
    dhidden = weight_b.astype(jnp.float32)[:, None] * proj
    dgate = (dhidden * upped * sig * (1.0 + gated * (1.0 - sig))).astype(jnp.bfloat16)
    dup = (dhidden * active).astype(jnp.bfloat16)
    back = lax.dot_general(dgate, gate, contract, preferred_element_type=jnp.float32)
    back = back + lax.dot_general(dup, up, contract, preferred_element_type=jnp.float32)
    scaled = (weight_b.astype(jnp.float32)[:, None] * cot.astype(jnp.float32)).astype(jnp.bfloat16)
    dweight = lax.dot_general(
        hidden, scaled, (((0,), (0,)), ((), ())), preferred_element_type=jnp.float32
    )
    return (dots, back.astype(jnp.bfloat16), dweight)


def widen(array, held_count):
    shape = array.shape
    grown = jnp.broadcast_to(array[:, None], (held_count, SPLIT) + shape[1:])
    return grown.reshape((held_count * SPLIT,) + shape[1:])


def per_device(tokens, cotangent, logits, expert_ids, gate_proj, up_proj, down_proj):
    devices = lax.axis_size("expert")
    held = devices // SPLIT
    tok_count, top = expert_ids.shape
    experts = logits.shape[1]
    width = tokens.shape[1]
    capacity = max(2, 5 * tok_count * top // (4 * experts))
    send_count = held * capacity
    slot_count = devices * capacity
    pick, chosen, total, weight = router_weights(logits, expert_ids)
    weight_b = weight.astype(jnp.bfloat16).reshape(-1)
    ranks = slot_ranks(expert_ids, experts)
    flat_ids = expert_ids.reshape(-1)
    inside = flat_ids < held
    position = jnp.where(inside, flat_ids * capacity + ranks, -1)
    match = (position[:, None] == jnp.arange(send_count, dtype=jnp.int32)[None, :]).astype(
        jnp.int32
    )
    filled = jnp.sum(match, axis=0) > 0
    source_entry = jnp.sum(match * jnp.arange(tok_count * top, dtype=jnp.int32)[:, None], axis=0)
    source_tok = source_entry // top
    zero_b = jnp.zeros((), jnp.bfloat16)
    rows_block = jnp.where(filled[:, None], tokens[source_tok], zero_b).reshape(
        held, capacity, width
    )
    cot_block = jnp.where(filled[:, None], cotangent[source_tok], zero_b).reshape(
        held, capacity, width
    )
    send_weight = widen(
        jnp.where(filled, weight_b[source_entry], zero_b).reshape(held, capacity), held
    )
    gate = gate_proj[0]
    up = up_proj[0]
    down = down_proj[0]
    send_rows = widen(rows_block, held)
    send_cot = widen(cot_block, held)
    got_rows, got_cot, got_weight = (
        lax.all_to_all(send_rows, "expert", split_axis=0, concat_axis=0, tiled=True),
        lax.all_to_all(send_cot, "expert", split_axis=0, concat_axis=0, tiled=True),
        lax.all_to_all(send_weight, "expert", split_axis=0, concat_axis=0, tiled=True),
    )
    forward = expert_forward(got_rows.reshape(slot_count, width), gate, up)
    cot_rows = got_cot.reshape(slot_count, width)
    dots, back, dweight = expert_backward(
        forward, cot_rows, got_weight.reshape(slot_count), gate, up, down
    )
    back_got, dots_got = (
        lax.all_to_all(
            back.reshape(devices, capacity, width),
            "expert",
            split_axis=0,
            concat_axis=0,
            tiled=True,
        ),
        lax.all_to_all(
            dots.reshape(devices, capacity), "expert", split_axis=0, concat_axis=0, tiled=True
        ),
    )
    per_token = jnp.sum(match.reshape(tok_count, top, send_count), axis=1).reshape(
        tok_count, held, capacity
    )
    combine = widen(jnp.transpose(per_token, (1, 0, 2)), held).reshape(
        held, SPLIT, tok_count, capacity
    )
    combine = (
        jnp.transpose(combine, (2, 0, 1, 3)).reshape(tok_count, slot_count).astype(jnp.bfloat16)
    )
    token_grad = jnp.dot(
        combine, back_got.reshape(slot_count, width), preferred_element_type=jnp.float32
    ).astype(jnp.bfloat16)
    dots_sum = jnp.sum(dots_got.astype(jnp.float32).reshape(held, SPLIT, capacity), axis=1).reshape(
        send_count
    )
    safe = jnp.where(inside, position, 0)
    dweight_tk = jnp.where(inside, dots_sum[safe], jnp.zeros((), jnp.float32)).reshape(
        tok_count, top
    )
    logit_grad = router_grad(pick, chosen, total, dweight_tk)
    down_part = lax.psum_scatter(dweight, "dp", scatter_dimension=1, tiled=True)
    down_grad = down_part.astype(jnp.bfloat16)[None]
    return (token_grad, logit_grad, down_grad)


def solution(mesh):
    in_specs = (
        P(("expert", "dp"), None),
        P(("expert", "dp"), None),
        P(("expert", "dp"), None),
        P(("expert", "dp"), None),
        P("expert", None, None),
        P("expert", None, None),
        P("expert", None, None),
    )
    out_specs = (P(("expert", "dp"), None), P(("expert", "dp"), None), P("expert", None, "dp"))
    return jax.shard_map(
        per_device, mesh=mesh, in_specs=in_specs, out_specs=out_specs, check_vma=False
    )
```

profile of v0, /device:TPU:1, one launch (start us, length us, event | category | flops | bytes accessed | tf_op | source)
XLA Modules:
  0.0 1164.7 jit_solution(7405118986034462142)
XLA Ops:
  14.8 16.3 %all-to-all-start = ((bf16[128,1,5]{2,1,0:T(2,128)(2,1)}), bf16[128,1,5]{2,1,0:T(2,128)(2,1)S(1)}, u32[]{:S(2)}, u32[]{:S(2)}) async-start(bf16[128,1,5]{2,1,0:T(2,128)(2,1)} %copy.57), calls=%async_computation | async-start | bytes 131072 | tf_op jit(solution)/shard_map/all_to_all | solution.py:107
  31.2 3.2 gather_fusion.2
  34.6 3.2 gather_fusion.1
  41.9 8.3 broadcast_in_dim.85
  50.1 331.9 %all_to_all.30 = bf16[128,5,7168]{2,1,0:T(8,128)(2,1)} all-to-all(bf16[128,5,7168]{2,1,0:T(8,128)(2,1)} %bitcast.105), channel_id=1, replica_groups=mesh['expert'=128,'dp'=2] {'expert'}, dimensions={0} | all-to-all | bytes 18350080 | tf_op jit(solution)/shard_map/all_to_all | solution.py:105
  382.0 7.1 broadcast_in_dim.84
  389.1 10.8 all-to-all-start.1
  400.3 15.1 %reshape.279 = bf16[640,7168]{1,0:T(8,128)(2,1)} reshape(bf16[128,5,7168]{2,1,0:T(8,128)(2,1)} %all_to_all.30) | data formatting | bytes 18350080 | tf_op jit(solution)/shard_map/reshape | solution.py:109
  415.4 6.5 fusion.4
  422.2 2.9 fusion.7
  425.0 301.6 %all-to-all-done.1 = bf16[128,5,7168]{2,1,0:T(8,128)(2,1)} async-done(((bf16[128,5,7168]{2,1,0:T(8,128)(2,1)}), bf16[128,5,7168]{2,1,0:T(8,128)(2,1)}, u32[]{:S(2)}, u32[]{:S(2)}) %all-to-all-start.1) | async-done | bytes 9175072 | tf_op jit(solution)/shard_map/all_to_all | solution.py:106
  726.6 15.1 %reshape.277 = bf16[640,7168]{1,0:T(8,128)(2,1)} reshape(bf16[128,5,7168]{2,1,0:T(8,128)(2,1)} %all-to-all-done.1) | data formatting | bytes 18350080 | tf_op jit(solution)/shard_map/reshape | solution.py:110
  741.7 7.1 multiply_reduce_fusion
  749.6 9.6 all-to-all-start.4
  759.3 8.9 fusion.2
  768.2 12.4 %add_convert_fusion = bf16[640,7168]{1,0:T(8,128)(2,1)} fusion(f32[640,7168]{1,0:T(8,128)} %fusion.2, bf16[1,7168,128]{2,1,0:T(8,128)(2,1)S(1)} %copy-done.4, f32[640,128]{0,1:T(8,128)S(1)} %get-tuple-element.93, f32[640]{0:T(1024)S(1)} %reshape.283, f32[640,128]{0,1:T(8,128)S(1)} %fusion.4), kind=kOutput, calls=%fused_computation.4 | convolution fusion | flops 1184153600 | bytes 30018048 | tf_op jit(solution)/shard_map/dot_general | solution.py:54
  780.6 14.8 %reshape.280 = bf16[128,5,7168]{2,1,0:T(8,128)(2,1)} reshape(bf16[640,7168]{1,0:T(8,128)(2,1)} %add_convert_fusion) | data formatting | bytes 18350080 | tf_op jit(solution)/shard_map/reshape | solution.py:116
  795.4 13.8 %all-to-all-start.3 = ((bf16[128,5,7168]{2,1,0:T(8,128)(2,1)}), bf16[128,5,7168]{2,1,0:T(8,128)(2,1)}, u32[]{:S(2)}, u32[]{:S(2)}) async-start(bf16[128,5,7168]{2,1,0:T(8,128)(2,1)} %reshape.280), calls=%async_computation.3 | async-start | bytes 29360128 | tf_op jit(solution)/shard_map/all_to_all | solution.py:115
  809.5 7.3 fusion
  820.1 4.6 compare_select_fusion.1
  825.1 21.5 %select_select_fusion.1 = f32[1024]{0:T(1024)S(1)} fusion(pred[1024]{0:T(1024)(128)(4,1)S(1)} %get-tuple-element.37, pred[1024]{0:T(1024)(128)(4,1)S(1)} %get-tuple-element.36, pred[1024]{0:T(1024)(128)(4,1)S(1)} %get-tuple-element.35, pred[1024]{0:T(1024)(128)(4,1)S(1)} %get-tuple-element.34, pred[1024]{0:T(1024)(128)(4,1)S(1)} %get-tuple-element.33, ...), kind=kLoop, calls=%fused_computation.96 | loop fusion | flops 33792 | bytes 42116 | tf_op jit(solution)/shard_map/gather | solution.py:142
  850.4 285.2 %all-to-all-done.3 = bf16[128,5,7168]{2,1,0:T(8,128)(2,1)} async-done(((bf16[128,5,7168]{2,1,0:T(8,128)(2,1)}), bf16[128,5,7168]{2,1,0:T(8,128)(2,1)}, u32[]{:S(2)}, u32[]{:S(2)}) %all-to-all-start.3) | async-done | bytes 9175072 | tf_op jit(solution)/shard_map/all_to_all | solution.py:115
  1135.7 15.2 %reshape.281 = bf16[640,7168]{1,0:T(8,128)(2,1)} reshape(bf16[128,5,7168]{2,1,0:T(8,128)(2,1)} %all-to-all-done.3) | data formatting | bytes 18350080 | tf_op jit(solution)/shard_map/reshape | solution.py:136
  1150.9 6.5 convolution_convert_fusion
  (81 shorter events, 21.1 us)
Async XLA Ops:
  7.2 408.3 %copy-start = (bf16[1,7168,128]{2,1,0:T(8,128)(2,1)S(1)}, bf16[1,7168,128]{2,1,0:T(8,128)(2,1)}, u32[]{:S(2)}) copy-start(bf16[1,7168,128]{2,1,0:T(8,128)(2,1)} %param.11) | copy-start | bytes 5505028
  14.8 27.0 %all-to-all-start = ((bf16[128,1,5]{2,1,0:T(2,128)(2,1)}), bf16[128,1,5]{2,1,0:T(2,128)(2,1)S(1)}, u32[]{:S(2)}, u32[]{:S(2)}) async-start(bf16[128,1,5]{2,1,0:T(2,128)(2,1)} %copy.57), calls=%async_computation | async-start | bytes 131072 | tf_op jit(solution)/shard_map/all_to_all | solution.py:107
  50.1 331.9 %copy-start.5 = (bf16[8,5,7168]{2,1,0:T(8,128)(2,1)S(1)}, bf16[8,5,7168]{2,1,0:T(8,128)(2,1)}, u32[]{:S(2)}) copy-start(bf16[8,5,7168]{2,1,0:T(8,128)(2,1)} %get-tuple-element.47) | copy-start | bytes 1720324
  389.1 337.5 %all-to-all-start.1 = ((bf16[128,5,7168]{2,1,0:T(8,128)(2,1)}), bf16[128,5,7168]{2,1,0:T(8,128)(2,1)}, u32[]{:S(2)}, u32[]{:S(2)}) async-start(bf16[128,5,7168]{2,1,0:T(8,128)(2,1)} %bitcast.104), calls=%async_computation.1 | async-start | bytes 29360128 | tf_op jit(solution)/shard_map/all_to_all | solution.py:106
  415.4 6.6 copy-start.2
  415.4 6.7 copy-start.3
  749.6 45.8 %all-to-all-start.4 = ((bf16[128,1,5]{2,1,0:T(2,128)(2,1)}), bf16[128,1,5]{2,1,0:T(2,128)(2,1)S(1)}, u32[]{:S(2)}, u32[]{:S(2)}) async-start(bf16[128,1,5]{2,1,0:T(2,128)(2,1)} %convert_element_type.128), calls=%async_computation.4 | async-start | bytes 131072 | tf_op jit(solution)/shard_map/all_to_all | solution.py:122
  759.3 8.9 copy-start.4
  795.4 340.2 %all-to-all-start.3 = ((bf16[128,5,7168]{2,1,0:T(8,128)(2,1)}), bf16[128,5,7168]{2,1,0:T(8,128)(2,1)}, u32[]{:S(2)}, u32[]{:S(2)}) async-start(bf16[128,5,7168]{2,1,0:T(8,128)(2,1)} %reshape.280), calls=%async_computation.3 | async-start | bytes 29360128 | tf_op jit(solution)/shard_map/all_to_all | solution.py:115
  809.2 38.7 %reduce-scatter.2.cloned.1.call-start = ((), (), s32[]{:S(2)}) async-start(), calls=%async_computation.6 | async-start | bytes 5505024 | tf_op jit(solution)/shard_map/reduce_scatter | solution.py:146
  809.5 7.6 copy-start.6
  1135.7 21.7 %copy-start.1 = (bf16[1,7168,128]{2,1,0:T(8,128)(2,1)S(1)}, bf16[1,7168,128]{2,1,0:T(8,128)(2,1)}, u32[]{:S(2)}) copy-start(bf16[1,7168,128]{2,1,0:T(8,128)(2,1)} %param.11) | copy-start | bytes 5505028
Sparse Core Ops, SparseCore 0:
  817.0 18.9 reduce-scatter.1
where the time goes:
time: 1180 us; the launch traced here: 1160 us
  waiting for transfers between devices  587 us (50%)
  blocking collectives  332 us (28%)
  local copies, waits for them, and re-layouts  91.5 us (8%)
  matrix products  51.6 us (4%)
  starting transfers between devices  50.9 us (4%)
  other arithmetic  36.9 us (3%)
  between operations  14.8 us (1%)
    all_to_all x1, blocking collectives, per_device(): lax.all_to_all(send_rows, 'expert', split_axis=0, concat_axis=0, tiled=True)  332 us
    all_to_all x1, waiting for transfers between devices, per_device(): lax.all_to_all(send_cot, 'expert', split_axis=0, concat_axis=0, tiled=True)  302 us
    all_to_all x1, waiting for transfers between devices, per_device(): lax.all_to_all(back.reshape(devices, capacity, width), 'expert', split_ax...  285 us
    gather x3, other arithmetic, per_device(): dots_sum[safe]  26.5 us
  transfers between devices with their start and end apart: 5, of which 3 were waited for; matrix products, arithmetic and copies ran while one was open for 10% of the time, Pallas kernels for 0%

commit v1 on v0

v1 whole, which is shorter than its diff:
```python
import jax
import jax.numpy as jnp
from jax import lax
from jax.experimental import pallas as pl
from jax.experimental.pallas import tpu as pltpu
from jax.sharding import PartitionSpec as P

NZ, NX, NY = 8, 4, 4
NS = NZ * NY
SCALE = 2.5
CAP = 5
SLOTS = NZ * CAP
PAD = 48
LAG = 4
MESH = pl.DeviceIdType.MESH
f32, bf16 = jnp.float32, jnp.bfloat16
NT = (((1,), (1,)), ((), ()))
TN = (((0,), (0,)), ((), ()))


def kernel(
    put_ref, putw_ref, take_ref, tok_hbm, cot_hbm, gate_hbm, up_hbm, down_hbm,
    tg_ref, dots_ref, dg_hbm,
    tok, cot, sendb, rx, xr, cr, wg, wu, wd, relay_g, relay_u, relay_d,
    part, own1, y1p, y1m, y2p, y2m, mid, bk, own2, x1p, x1m, x2p, x2m,
    retb, fin, dd, dsend, drecv, dout,
    lsem, wlsem, sem_a, sem_bp, sem_bm, sem_cp, sem_cm, wsem, rsem, psem,
    ysem, msem, xsem, fsem, ssem, dsem, osem,
):
    wide = xr.shape[1]
    half = wide // 2
    ffd = gate_hbm.shape[1]
    rows = NS * CAP
    e = lax.axis_index("expert")
    c = lax.axis_index("dp")
    z, x, y = e // (NX * NY), (e // NY) % NX, e % NY
    other = 1 - c
    at = lambda zz, xx, yy: zz * (NX * NY) + xx * NY + yy
    yp, ym, y2 = (y + 1) % NY, (y + 3) % NY, (y + 2) % NY
    xp, xm, x2 = (x + 1) % NX, (x + 3) % NX, (x + 2) % NX
    me = z * NY + y
    dev_yp, dev_ym = at(z, x, yp), at(z, x, ym)
    dev_xp, dev_xm = at(z, xp, y), at(z, xm, y)

    def remote(src, dst, recv, ex, dp=c):
        return pltpu.make_async_remote_copy(
            src_ref=src, dst_ref=dst, send_sem=ssem.at[0], recv_sem=recv,
            device_id=(ex, dp), device_id_type=MESH,
        )

    sent = []

    def send(src, dst, recv, ex, dp=c):
        cp = remote(src, dst, recv, ex, dp)
        cp.start()
        sent.append(cp)

    def arrived(dst, recv):
        remote(dst, dst, recv, dev_yp).wait_recv()

    ld_t = pltpu.make_async_copy(tok_hbm, tok, lsem.at[0])
    ld_c = pltpu.make_async_copy(cot_hbm, cot, lsem.at[1])
    ld_t.start()
    ld_c.start()
    r_own = pl.ds(pl.multiple_of(y * wide, wide), wide)
    l_own = pl.ds(pl.multiple_of(y * ffd, ffd), ffd)
    w_loads = [
        pltpu.make_async_copy(gate_hbm.at[r_own], wg.at[:, l_own], wlsem.at[0]),
        pltpu.make_async_copy(up_hbm.at[r_own], wu.at[:, l_own], wlsem.at[1]),
        pltpu.make_async_copy(down_hbm.at[:, r_own], wd.at[l_own], wlsem.at[2]),
    ]
    for cp in w_loads:
        cp.start()

    barrier = pltpu.get_barrier_semaphore()

    def greet(ex, dp):
        pl.semaphore_signal(barrier, inc=1, device_id=(ex, dp), device_id_type=MESH)

    @pl.loop(1, NS)
    def _(d):
        greet(at((z + d // NY) % NZ, x, (y + d % NY) % NY), c)

    greet(dev_xp, c)
    greet(dev_xm, c)
    for d in range(NY):
        greet(at(z, x, (y + d) % NY), other)

    fin[:, SLOTS:PAD] = jnp.zeros((NY, PAD - SLOTS, 2, fin.shape[3]), bf16)
    ld_t.wait()
    ld_c.wait()
    for yy in range(NY):
        cols = slice(yy * wide, (yy + 1) * wide)
        v = jnp.dot(put_ref[...], tok[:, cols], preferred_element_type=f32).astype(bf16)
        sendb[yy, 0] = v.reshape(PAD, 2, half)
        v = jnp.dot(putw_ref[...], cot[:, cols], preferred_element_type=f32).astype(bf16)
        sendb[yy, 1] = v.reshape(PAD, 2, half)

    pl.semaphore_wait(barrier, NS - 1 + 2 + NY)

    def a_copy(d):
        zz, yy = (z + d // NY) % NZ, (y + d % NY) % NY
        return remote(
            sendb.at[yy, :, pl.ds(zz * CAP, CAP)], rx.at[:, x, pl.ds(me * CAP, CAP)],
            sem_a.at[me], at(zz, x, yy),
        )

    own = pltpu.make_async_copy(
        sendb.at[y, :, pl.ds(z * CAP, CAP)], rx.at[:, x, pl.ds(me * CAP, CAP)], sem_a.at[me]
    )
    own.start()

    @pl.loop(1, NS)
    def _(d):
        a_copy(d).start()

    h = pl.ds(pl.multiple_of(c * half, half), half)

    def src_of(yy):
        r = pl.ds(pl.multiple_of(yy * wide + c * half, half), half)
        return (gate_hbm.at[r], up_hbm.at[r], down_hbm.at[:, r])

    def dst_of(yy, hh):
        l = pl.ds(pl.multiple_of(yy * ffd, ffd), ffd)
        return (wg.at[hh, l], wu.at[hh, l], wd.at[l, hh])

    relays = (relay_g, relay_u, relay_d)
    via = jnp.where(c == 0, dev_yp, dev_ym)
    came = jnp.where(c == 0, ym, yp)
    for i, s in enumerate(src_of(y2)):
        send(s, relays[i], rsem.at[i], via)
    for i, s in enumerate(src_of(yp)):
        send(s, dst_of(y, h)[i], wsem.at[y, i], dev_yp)
    for i, s in enumerate(src_of(ym)):
        send(s, dst_of(y, h)[i], wsem.at[y, i], dev_ym)

    def src_at(d):
        s = ((z + NZ - d // NY) % NZ) * NY + (y + NY - d % NY) % NY
        return s, pl.ds(s * CAP, CAP)

    def b_copies(d):
        s, r = src_at(d)
        blk = rx.at[:, x, r]
        return remote(blk, blk, sem_bp.at[s], dev_xp), remote(blk, blk, sem_bm.at[s], dev_xm)

    def c_copies(d):
        s, r = src_at(d)
        pb, mb = rx.at[0, xm, r], rx.at[1, xp, r]
        return remote(pb, pb, sem_cp.at[s], dev_xp), remote(mb, mb, sem_cm.at[s], dev_xm)

    def start_b(d):
        for cp in b_copies(d):
            cp.start()

    def start_c(d):
        s, r = src_at(d)
        arrived(rx.at[:, xm, r], sem_bp.at[s])
        arrived(rx.at[:, xp, r], sem_bm.at[s])
        for cp in c_copies(d):
            cp.start()

    def wait_a(d):
        s, r = src_at(d)
        arrived(rx.at[:, x, r], sem_a.at[s])

    own.wait()
    start_b(0)

    @pl.loop(1, LAG)
    def _(d):
        wait_a(d)
        start_b(d)

    @pl.loop(LAG, NS // 2)
    def _(d):
        wait_a(d)
        start_b(d)
        start_c(d - LAG)

    for i in range(3):
        arrived(relays[i], rsem.at[i])
        send(relays[i], dst_of(came, h)[i], wsem.at[came, i], via)

    @pl.loop(NS // 2, NS)
    def _(d):
        wait_a(d)
        start_b(d)
        start_c(d - LAG)

    @pl.loop(NS - LAG, NS)
    def _(d):
        start_c(d)

    for yy in (yp, ym, y2):
        for i in range(3):
            blk = dst_of(yy, h)[i]
            arrived(blk, wsem.at[yy, i])
            send(blk, blk, psem.at[yy, i], e, other)

    @pl.loop(0, NS)
    def _(d):
        s, r = src_at(d)
        arrived(rx.at[0, x2, r], sem_cp.at[s])
        arrived(rx.at[1, x2, r], sem_cm.at[s])

    @pl.loop(0, rows // 16)
    def _(i):
        r = pl.ds(i * 16, 16)
        for k in range(NX):
            o = pl.ds(pl.multiple_of(k * rows + i * 16, 16), 16)
            xr[o] = rx[0, k, r].reshape(16, wide)
            cr[o] = rx[1, k, r].reshape(16, wide)

    ho = pl.ds(pl.multiple_of(other * half, half), half)
    for cp in w_loads:
        cp.wait()
    for yy in (yp, ym, y2):
        for i in range(3):
            arrived(dst_of(yy, ho)[i], psem.at[yy, i])

    def reduce_scatter(compute, part, own_ref, hh, pos, dev_p, dev_m, b1p, b1m, b2p, b2m, sems, between):
        kp, km, kf = (pos + 1) % 4, (pos + 3) % 4, (pos + 2) % 4
        lo, hi = slice(0, hh), slice(hh, part.shape[2])
        compute(kf, None)
        send(part.at[kf, :, lo], b1p, sems.at[0], dev_p)
        send(part.at[kf, :, hi], b1m, sems.at[1], dev_m)
        compute(kp, None)
        send(part.at[kp, :, hi], b2p.at[:, hi], sems.at[2], dev_p)
        compute(km, None)
        send(part.at[km, :, lo], b2m.at[:, lo], sems.at[3], dev_m)
        compute(pos, own_ref)
        arrived(b1p, sems.at[0])
        part[kp, :, lo] = (part[kp, :, lo].astype(f32) + b1p[...].astype(f32)).astype(bf16)
        send(part.at[kp, :, lo], b2p.at[:, lo], sems.at[4], dev_p)
        arrived(b1m, sems.at[1])
        part[km, :, hi] = (part[km, :, hi].astype(f32) + b1m[...].astype(f32)).astype(bf16)
        send(part.at[km, :, hi], b2m.at[:, hi], sems.at[5], dev_m)
        between()
        arrived(b2p.at[:, hi], sems.at[2])
        arrived(b2m.at[:, lo], sems.at[3])
        arrived(b2p.at[:, lo], sems.at[4])
        arrived(b2m.at[:, hi], sems.at[5])

    ff = wg.shape[1]

    def forward(k, keep):
        r = pl.ds(pl.multiple_of(k * rows, 16), rows)
        xv, cv = xr[r], cr[r]
        vals = (
            jnp.dot(xv, wg[...], preferred_element_type=f32),
            jnp.dot(xv, wu[...], preferred_element_type=f32),
            lax.dot_general(cv, wd[...], NT, preferred_element_type=f32),
        )
        for i, v in enumerate(vals):
            if keep is None:
                part[k, :, i * ff : (i + 1) * ff] = v.astype(bf16)
            else:
                keep[:, i * ff : (i + 1) * ff] = v

    reduce_scatter(
        forward, part, own1, 3 * ff // 2, y, dev_yp, dev_ym, y1p, y1m, y2p, y2m, ysem, lambda: None
    )

    @pl.loop(0, rows // 16)
    def _(i):
        r = pl.ds(pl.multiple_of(i * 16, 16), 16)
        full = own1[r] + y2p[r].astype(f32) + y2m[r].astype(f32)
        g, u, pw = full[:, :ff], full[:, ff : 2 * ff], full[:, 2 * ff :]
        sig = jax.nn.sigmoid(g)
        act = g * sig
        hid = (act * u).astype(bf16)
        prod = hid.astype(f32) * pw
        lanes = prod[:, :128]
        for k in range(1, ff // 128):
            lanes = lanes + prod[:, k * 128 : (k + 1) * 128]
        mid[y, r, 0:ff] = hid
        mid[y, r, ff : 2 * ff] = (pw * u * sig * (1.0 + g * (1.0 - sig))).astype(bf16)
        mid[y, r, 2 * ff : 3 * ff] = (pw * act).astype(bf16)
        mid[y, r, 3 * ff : 3 * ff + 128] = lanes.astype(bf16)

    ca, cb = slice(0, 896), slice(896, mid.shape[2])
    block = lambda k, cols: mid.at[k, :, cols]
    send(block(y, ca), block(y, ca), msem.at[0], dev_yp)
    send(block(y, cb), block(y, cb), msem.at[1], dev_ym)
    send(block(y, cb), block(y, cb), msem.at[2], dev_yp)
    send(block(y, ca), block(y, ca), msem.at[3], dev_ym)
    arrived(block(ym, ca), msem.at[0])
    send(block(ym, ca), block(ym, ca), msem.at[4], dev_yp)
    arrived(block(yp, cb), msem.at[1])
    send(block(yp, cb), block(yp, cb), msem.at[5], dev_ym)
    arrived(block(ym, cb), msem.at[2])
    arrived(block(yp, ca), msem.at[3])
    arrived(block(y2, ca), msem.at[4])
    arrived(block(y2, cb), msem.at[5])

    def backward(k, keep):
        v = lax.dot_general(mid[k, :, ff : 2 * ff], wg[...], NT, preferred_element_type=f32)
        v = v + lax.dot_general(mid[k, :, 2 * ff : 3 * ff], wu[...], NT, preferred_element_type=f32)
        lanes = mid[k, :, 3 * ff : 3 * ff + 128]
        if keep is None:
            bk[k, :, :wide] = v.astype(bf16)
            bk[k, :, wide:] = lanes
        else:
            keep[:, :wide] = v
            keep[:, wide:] = lanes.astype(f32)

    mine = pl.ds(pl.multiple_of(c * (ff // 2), ff // 2), ff // 2)
    theirs = pl.ds(pl.multiple_of(other * (ff // 2), ff // 2), ff // 2)

    def down_part():
        for n in range(0, wide, 256):
            cols = slice(n, n + 256)
            acc = None
            for k in range(NX):
                v = lax.dot_general(
                    mid[k, :, 0:ff], cr[k * rows : (k + 1) * rows, cols], TN, preferred_element_type=f32
                )
                acc = v if acc is None else acc + v
            dd[:, cols] = acc
        dsend[...] = dd[theirs].astype(bf16)
        send(dsend, drecv, dsem.at[0], e, other)
        arrived(drecv, dsem.at[0])
        dout[...] = (dd[mine] + drecv[...].astype(f32)).astype(bf16)

    reduce_scatter(
        backward, bk, own2, 1024, x, dev_xp, dev_xm, x1p, x1m, x2p, x2m, xsem, down_part
    )

    @pl.loop(0, rows // 16)
    def _(i):
        r = pl.ds(pl.multiple_of(i * 16, 16), 16)
        full = own2[r] + x2p[r].astype(f32) + x2m[r].astype(f32)
        retb[pl.ds(i * 16, 16), :, 0:half] = full[:, :wide].astype(bf16).reshape(16, 2, half)
        lanes = jnp.concatenate([full[:, wide:], jnp.zeros((16, 128), f32)], axis=1).astype(bf16)
        retb[pl.ds(i * 16, 16), :, half : half + 128] = lanes.reshape(16, 2, 128)

    def f_copy(d):
        zz, yy = (z + d // NY) % NZ, (y + d % NY) % NY
        return remote(
            retb.at[pl.ds((zz * NY + yy) * CAP, CAP)], fin.at[y, pl.ds(z * CAP, CAP)],
            fsem.at[me], at(zz, x, yy),
        )

    back_own = pltpu.make_async_copy(
        retb.at[pl.ds(me * CAP, CAP)], fin.at[y, pl.ds(z * CAP, CAP)], fsem.at[me]
    )
    back_own.start()

    @pl.loop(1, NS)
    def _(d):
        f_copy(d).start()

    to_core = y // 2
    o_cols = pl.ds(pl.multiple_of((y % 2) * wide, wide), wide)
    for i in range(2):
        yy = 2 * c + i
        src = dout.at[pl.ds(i * ffd, ffd)]
        here = (yy == y) & (to_core == c)

        @pl.when(here)
        def _():
            pltpu.make_async_copy(src, dg_hbm.at[0, :, o_cols], osem.at[y % 2]).start()

        @pl.when(jnp.logical_not(here))
        def _():
            remote(src, dg_hbm.at[0, :, o_cols], osem.at[y % 2], at(z, x, yy), to_core).start()

    back_own.wait()

    @pl.loop(1, NS)
    def _(d):
        zz, yy = (z + NZ - d // NY) % NZ, (y + NY - d % NY) % NY
        arrived(fin.at[yy, pl.ds(zz * CAP, CAP)], fsem.at[zz * NY + yy])

    for yy in range(NY):
        v = fin[yy, :, :, 0:half].reshape(PAD, wide)
        tg_ref[:, yy * wide : (yy + 1) * wide] = jnp.dot(
            take_ref[...], v, preferred_element_type=f32
        ).astype(bf16)
    dots_ref[...] = fin[0, :, :, half : half + 128].reshape(PAD, 256)[:, :128].astype(f32)

    for i in range(2):
        arrived(dg_hbm.at[0, :, i * wide : (i + 1) * wide], osem.at[i])
    for cp in sent:
        cp.wait_send()

    @pl.loop(1, NS)
    def _(d):
        a_copy(d).wait_send()
        f_copy(d).wait_send()

    @pl.loop(0, NS)
    def _(d):
        for cp in (*b_copies(d), *c_copies(d)):
            cp.wait_send()

    for i in range(2):
        yy = 2 * c + i

        @pl.when(jnp.logical_not((yy == y) & (to_core == c)))
        def _():
            remote(dout.at[pl.ds(i * ffd, ffd)], dg_hbm.at[0, :, o_cols], osem.at[y % 2], at(z, x, yy), to_core).wait_send()


def exchange(put, putw, take, tokens, cotangent, gate, up, down):
    tok_count, width = tokens.shape
    ffd = gate.shape[1]
    wide, ff, rows = width // NY, NY * ffd, NS * CAP
    half = wide // 2
    n = NX * rows
    vm = pltpu.VMEM
    dma = pltpu.SemaphoreType.DMA
    scratch = [
        vm((tok_count, width), bf16), vm((tok_count, width), bf16),
        vm((NY, 2, PAD, 2, half), bf16), vm((2, NX, rows, 2, half), bf16),
        vm((n, wide), bf16), vm((n, wide), bf16),
        vm((wide, ff), bf16), vm((wide, ff), bf16), vm((ff, wide), bf16),
        vm((half, ffd), bf16), vm((half, ffd), bf16), vm((ffd, half), bf16),
        vm((NY, rows, 3 * ff), bf16), vm((rows, 3 * ff), f32),
        vm((rows, 3 * ff // 2), bf16), vm((rows, 3 * ff // 2), bf16),
        vm((rows, 3 * ff), bf16), vm((rows, 3 * ff), bf16),
        vm((NY, rows, 3 * ff + 128), bf16),
        vm((NX, rows, wide + 128), bf16), vm((rows, wide + 128), f32),
        vm((rows, 1024), bf16), vm((rows, wide + 128 - 1024), bf16),
        vm((rows, wide + 128), bf16), vm((rows, wide + 128), bf16),
        vm((rows, 2, half + 128), bf16), vm((NY, PAD, 2, half + 128), bf16),
        vm((ff, wide), f32), vm((ff // 2, wide), bf16), vm((ff // 2, wide), bf16), vm((ff // 2, wide), bf16),
        dma((2,)), dma((3,)), dma((NS,)), dma((NS,)), dma((NS,)), dma((NS,)), dma((NS,)),
        dma((NY, 3)), dma((3,)), dma((NY, 3)),
        dma((6,)), dma((6,)), dma((6,)), dma((NS,)), dma((1,)), dma((1,)), dma((2,)),
    ]
    v, a = pl.BlockSpec(memory_space=pltpu.VMEM), pl.BlockSpec(memory_space=pl.ANY)
    return pl.pallas_call(
        kernel,
        out_shape=(
            jax.ShapeDtypeStruct((tok_count, width), bf16),
            jax.ShapeDtypeStruct((PAD, 128), f32),
            jax.ShapeDtypeStruct((1, ffd, width // 2), bf16),
        ),
        in_specs=[v, v, v, a, a, a, a, a],
        out_specs=(v, v, a),
        scratch_shapes=scratch,
        compiler_params=pltpu.CompilerParams(
            collective_id=0, has_side_effects=True, vmem_limit_bytes=63 * 1024 * 1024
        ),
    )(put, putw, take, tokens, cotangent, gate, up, down)


def per_device(tokens, cotangent, logits, expert_ids, gate_proj, up_proj, down_proj):
    tok_count = expert_ids.shape[0]
    experts = logits.shape[1]
    pick = (expert_ids[:, :, None] == jnp.arange(experts, dtype=jnp.int32)[None, None, :]).astype(f32)
    chosen = jnp.sum(pick * jax.nn.sigmoid(logits)[:, None, :], axis=2)
    total = jnp.sum(chosen, axis=1, keepdims=True)
    weight_b = (SCALE * chosen / total).astype(bf16)
    live = expert_ids[:, :, None] == jnp.arange(NZ, dtype=jnp.int32)[None, None, :]
    member = jnp.any(live, axis=1)
    w_te = jnp.sum(jnp.where(live, weight_b.astype(f32)[:, :, None], 0.0), axis=1)
    rank = jnp.dot(jnp.tril(jnp.ones((tok_count, tok_count), f32), -1), member.astype(f32))
    place = member[:, :, None] & (rank[:, :, None] == jnp.arange(CAP, dtype=f32)[None, None, :])
    place = place.reshape(tok_count, SLOTS)
    place_f = jnp.pad(place.astype(f32), ((0, 0), (0, PAD - SLOTS)))
    place_w = jnp.pad(
        jnp.where(place, jnp.repeat(w_te, CAP, axis=1), 0.0), ((0, 0), (0, PAD - SLOTS))
    )
    token_grad, lanes, dd = exchange(
        place_f.T.astype(bf16), place_w.T.astype(bf16), place_f.astype(bf16),
        tokens, cotangent, gate_proj[0], up_proj[0], down_proj[0],
    )
    dots = jnp.sum(lanes, axis=1)[:SLOTS].reshape(NZ, CAP)
    d_te = jnp.sum(place.astype(f32).reshape(tok_count, NZ, CAP) * dots[None], axis=2)
    dweight = jnp.sum(jnp.where(live, d_te[:, None, :], 0.0), axis=2) / weight_b.astype(f32)
    inner = jnp.sum(dweight * chosen, axis=1, keepdims=True) / total
    dchosen = SCALE / total * (dweight - inner)
    logit_grad = jnp.sum(pick * (dchosen * chosen * (1.0 - chosen))[:, :, None], axis=1)
    return token_grad, logit_grad, dd


def solution(mesh):
    rows = P(("expert", "dp"), None)
    mats = P("expert", None, None)
    return jax.shard_map(
        per_device,
        mesh=mesh,
        in_specs=(rows, rows, rows, rows, mats, mats, mats),
        out_specs=(rows, rows, P("expert", None, "dp")),
        check_vma=False,
    )
```

time: 1180 us -> 165 us (0.14); the launches traced: 1160 us -> 163 us
  waiting for transfers between devices: 587 us -> 0 us
  blocking collectives: 332 us -> 0 us
  Pallas kernels: 0 us -> 148 us
  local copies, waits for them, and re-layouts: 91.5 us -> 6.76 us
  matrix products: 51.6 us -> 0.2 us
  starting transfers between devices: 50.9 us -> 0 us
  other arithmetic: 36.9 us -> 7.09 us
  between operations: 14.8 us -> 0.74 us
    all_to_all x4 -> x0, waiting for transfers between devices: 587 us -> none  [the longest x1 302 us: per_device(): lax.all_to_all(send_cot, 'expert', split_axis=0, concat_axis=0, tiled=True)]
    all_to_all x1 -> x0, blocking collectives: 332 us -> none  [per_device(): lax.all_to_all(send_rows, 'expert', split_axis=0, concat_axis=0, tiled=True)]
    pallas_call x0 -> x1, Pallas kernels: none -> 148 us  [exchange(): pl.pallas_call(kernel, out_shape=(jax.ShapeDtypeStruct((tok_count, width)...]
    reshape x5 -> x2, local copies, waits for them, and re-layouts: 60.3 us -> 0.14 us  [per_device(): jnp.repeat(w_te, CAP, axis=1)]
    dot_general x7 -> x1, matrix products: 51.6 us -> 0.2 us  [per_device(): jnp.dot(jnp.tril(jnp.ones((tok_count, tok_count), f32), -1), member.astyp...]
    all_to_all x4 -> x0, starting transfers between devices: 50.6 us -> none  [the longest x1 16.3 us: per_device(): lax.all_to_all(send_weight, 'expert', split_axis=0, concat_axis=0, tiled=...]
    gather x4 -> x0, other arithmetic: 26.5 us -> none  [the longest x3 26.5 us: per_device(): dots_sum[safe]]
    broadcast_in_dim x3 -> x1, local copies, waits for them, and re-layouts: 15.4 us -> 0.01 us  [per_device(): jnp.repeat(w_te, CAP, axis=1)]
  transfers between devices with their start and end apart: 5 -> 0, of which waited for: 3 -> 0; matrix products, arithmetic and copies ran while one was open for 10% -> 0% of each run, Pallas kernels for 0% -> 0%
where the time goes in v1:
time: 165 us; the launch traced here: 163 us
  Pallas kernels  148 us (90%)
  other arithmetic  7.09 us (4%)
  local copies, waits for them, and re-layouts  6.76 us (4%)
    pallas_call x1, Pallas kernels, exchange(): pl.pallas_call(kernel, out_shape=(jax.ShapeDtypeStruct((tok_count, width)...  148 us
    unnamed x7, local copies, waits for them, and re-layouts  4.65 us

profile of v1, /device:TPU:1, one launch (start us, length us, event | category | flops | bytes accessed | tf_op | source)
XLA Modules:
  0.0 163.3 jit_solution(17673097462299017016)
XLA Ops:
  0.6 0.7 fusion.5
  1.3 0.2 fusion
  1.5 0.1 eq.57
  1.7 0.1 copy.40
  1.8 0.1 copy.39
  1.9 0.8 copy.41
  2.7 0.9 add_divide_fusion
  3.7 2.0 %select_reduce_fusion = (f32[128]{0:T(128)S(1)}, f32[128,8]{1,0:T(8,128)S(1)}) fusion(f32[128,256]{1,0:T(8,128)S(1)} %add_divide_fusion, s32[128,8]{1,0:T(8,128)S(1)} %copy.41), kind=kLoop, calls=%fused_computation | loop fusion | flops 1047424 | bytes 139776 | tf_op jit(solution)/shard_map/reduce_sum | solution.py:454
  5.7 0.7 select_reduce_fusion.5
  6.5 0.1 copy.43
  6.7 0.7 copy.45.putw_ref
  7.3 0.6 convert_convert_fusion
  8.0 0.7 copy.44.put_ref
  8.7 0.0 copy-start.1
  8.7 148.5 %shard_map.94 = (bf16[128,7168]{1,0:T(8,128)(2,1)}, f32[48,128]{1,0:T(8,128)}, bf16[1,128,3584]{2,1,0:T(8,128)(2,1)}) custom-call(bf16[48,128]{1,0:T(8,128)(2,1)} %copy.44.put_ref, bf16[48,128]{1,0:T(8,128)(2,1)} %copy.45.putw_ref, bf16[128,48]{1,0:T(8,128)(2,1)} %get-tuple-element.15.take_ref, bf16[128,7168]{1,0:T(8,128)(2,1)} %tok_hbm.1, ...), custom_call_target="tpu_custom_call" | custom-call | tf_op jit(solution)/shard_map/pallas_call | solution.py:433
  157.1 0.8 reduce_sum.75
  158.0 0.1 mul.73
  158.1 0.1 select_reduce_fusion.4
  158.2 0.0 copy-done.1
  158.2 0.1 copy.49
  158.4 1.0 select_reduce_fusion.2
  159.4 2.9 %copy.52 = bf16[128,7168]{1,0:T(8,128)(2,1)} copy(bf16[128,7168]{1,0:T(8,128)(2,1)} %get-tuple-element.22) | data formatting | bytes 3670016
  162.3 0.0 copy-done
  162.3 0.9 copy.53
  (17 shorter events, 0.2 us)
Async XLA Ops:
  8.7 149.5 %copy-start.1 = (s32[128,8]{0,1:T(8,128)S(1)}, s32[128,8]{0,1:T(8,128)}, u32[]{:S(2)}) copy-start(s32[128,8]{0,1:T(8,128)} %param.10) | copy-start | bytes 12292
  159.4 2.9 %copy-start = (bf16[1,128,3584]{2,1,0:T(8,128)(2,1)S(1)}, bf16[1,128,3584]{2,1,0:T(8,128)(2,1)}, u32[]{:S(2)}) copy-start(bf16[1,128,3584]{2,1,0:T(8,128)(2,1)} %get-tuple-element.24) | copy-start | bytes 2752516

commit v2 on v1

v2 whole, which is shorter than its diff:
```python
import jax
import jax.numpy as jnp
from jax import lax
from jax.experimental import pallas as pl
from jax.experimental.pallas import tpu as pltpu
from jax.sharding import PartitionSpec as P

NZ, NX, NY = 8, 4, 4
NS = NZ * NY
SCALE = 2.5
CAP = 5
SLOTS = NZ * CAP
PAD = 48
LAG = 4
NB = 2
STOP = 99
MESH = pl.DeviceIdType.MESH
f32, bf16 = jnp.float32, jnp.bfloat16
NT = (((1,), (1,)), ((), ()))
TN = (((0,), (0,)), ((), ()))


def z_step(q):
    return jnp.where(q % 2 == 1, (q + 1) // 2, (NZ - q // 2) % NZ)


def iota(shape, dim):
    return lax.broadcasted_iota(jnp.int32, shape, dim)


def slot_map():
    e, s = iota((128, 128), 0), iota((128, 128), 1)
    return ((s >= CAP * e) & (s < CAP * (e + 1)) & (e < NZ)).astype(f32).astype(bf16)


def weights_of(named, total):
    return jnp.where(named > 0.0, SCALE * named / total, 0.0).astype(bf16)


def router(logits_ref, ids_ref):
    rows = logits_ref.shape[0]
    ids = jnp.transpose(ids_ref[...].astype(f32))
    lanes = iota(logits_ref.shape, 1).astype(f32)
    hit = lanes == ids[:, 0:1]
    for k in range(1, ids.shape[1]):
        hit = hit | (lanes == ids[:, k : k + 1])
    named = jnp.where(hit, jax.nn.sigmoid(logits_ref[...]), 0.0)
    total = jnp.sum(named, axis=1, keepdims=True)
    held = named[:, :128]
    slots = slot_map()
    member = jnp.dot((held > 0.0).astype(f32).astype(bf16), slots, preferred_element_type=f32)
    spread = jnp.dot(weights_of(held, total), slots, preferred_element_type=f32)
    earlier = (iota((rows, rows), 0) > iota((rows, rows), 1)).astype(f32).astype(bf16)
    rank = jnp.dot(earlier, member.astype(bf16), preferred_element_type=f32)
    lane = iota((rows, 128), 1)
    first = jnp.zeros((rows, 128), jnp.int32)
    for j in range(1, NZ):
        first = first + CAP * (lane >= CAP * j).astype(jnp.int32)
    place = jnp.where(rank == (lane - first).astype(f32), member, 0.0)
    return named, total, place, place * spread


def kernel(
    logits_ref, ids_ref, tok_hbm, cot_hbm, gate_hbm, up_hbm, down_hbm,
    named_ref, total_ref, take_ref, fin, dg_hbm,
    tok, cot, sendb, rx, xr, cr, wg, wu, wd, relay_g, relay_u, relay_d,
    part, y1p, y1m, y2p, y2m, mid, bk, x1p, x1m, x2p, x2m,
    retb, dl, dt, dd, dsend, drecv, dout,
    lsem, wlsem, sem_a, sem_bp, sem_bm, sem_cp, sem_cm, wsem, rsem, psem,
    ysem, msem, xsem, fsem, ssem, dsem, osem, tsem,
):
    wide = xr.shape[1]
    half = wide // 2
    ffd = gate_hbm.shape[1]
    ff = wg.shape[1]
    rows = NS * CAP
    step = rows // NB
    batch = NX * step
    e = lax.axis_index("expert")
    c = lax.axis_index("dp")
    z, x, y = e // (NX * NY), (e // NY) % NX, e % NY
    other = 1 - c
    at = lambda zz, xx, yy: zz * (NX * NY) + xx * NY + yy
    yp, ym, y2 = (y + 1) % NY, (y + 3) % NY, (y + 2) % NY
    xp, xm, x2 = (x + 1) % NX, (x + 3) % NX, (x + 2) % NX
    dev_yp, dev_ym = at(z, x, yp), at(z, x, ym)
    dev_xp, dev_xm = at(z, xp, y), at(z, xm, y)
    dev_t = at(z, y, x)

    def remote(src, dst, recv, ex, dp=c):
        return pltpu.make_async_remote_copy(
            src_ref=src, dst_ref=dst, send_sem=ssem.at[0], recv_sem=recv,
            device_id=(ex, dp), device_id_type=MESH,
        )

    sent = []

    def send(src, dst, recv, ex, dp=c):
        cp = remote(src, dst, recv, ex, dp)
        cp.start()
        sent.append(cp)

    def arrived(dst, recv):
        remote(dst, dst, recv, dev_yp).wait_recv()

    ld_t = pltpu.make_async_copy(tok_hbm, tok, lsem.at[0])
    ld_c = pltpu.make_async_copy(cot_hbm, cot, lsem.at[1])
    ld_t.start()
    ld_c.start()

    barrier = pltpu.get_barrier_semaphore()

    def greet(ex, dp):
        pl.semaphore_signal(barrier, inc=1, device_id=(ex, dp), device_id_type=MESH)

    @pl.loop(1, NS)
    def _(d):
        greet(at((z + d // NY) % NZ, x, (y + d % NY) % NY), c)

    greet(dev_xp, c)
    greet(dev_xm, c)
    for d in range(NY):
        greet(at(z, x, (y + d) % NY), other)

    @pl.when(x != y)
    def _():
        greet(dev_t, c)

    r_own = pl.ds(pl.multiple_of(y * wide, wide), wide)
    l_own = pl.ds(pl.multiple_of(y * ffd, ffd), ffd)
    w_loads = [
        pltpu.make_async_copy(gate_hbm.at[r_own], wg.at[:, l_own], wlsem.at[0]),
        pltpu.make_async_copy(up_hbm.at[r_own], wu.at[:, l_own], wlsem.at[1]),
        pltpu.make_async_copy(down_hbm.at[:, r_own], wd.at[l_own], wlsem.at[2]),
    ]
    for cp in w_loads:
        cp.start()

    named, total, place, place_w = router(logits_ref, ids_ref)
    named_ref[...] = named
    total_ref[...] = jnp.broadcast_to(total, total_ref.shape)
    take_ref[...] = place.astype(bf16)
    put, put_w = place[:, :PAD].astype(bf16), place_w[:, :PAD].astype(bf16)
    pl.semaphore_wait(barrier, NS - 1 + 2 + NY + jnp.where(x == y, 0, 1))

    h = pl.ds(pl.multiple_of(c * half, half), half)

    def src_of(yy):
        r = pl.ds(pl.multiple_of(yy * wide + c * half, half), half)
        return (gate_hbm.at[r], up_hbm.at[r], down_hbm.at[:, r])

    def dst_of(yy, hh):
        l = pl.ds(pl.multiple_of(yy * ffd, ffd), ffd)
        return (wg.at[hh, l], wu.at[hh, l], wd.at[l, hh])

    relays = (relay_g, relay_u, relay_d)
    via = jnp.where(c == 0, dev_yp, dev_ym)
    came = jnp.where(c == 0, ym, yp)
    send(src_of(y2)[2], relays[2], rsem.at[2], via)
    ld_t.wait()
    ld_c.wait()
    for yy in range(NY):
        cols = slice(yy * wide, (yy + 1) * wide)
        v = lax.dot_general(put, tok[:, cols], TN, preferred_element_type=f32).astype(bf16)
        sendb[yy, 0] = v[:SLOTS].reshape(SLOTS, 2, half)
        v = lax.dot_general(put_w, cot[:, cols], TN, preferred_element_type=f32).astype(bf16)
        sendb[yy, 1] = v[:SLOTS].reshape(SLOTS, 2, half)

    def a_copy(d):
        q = d // NY
        zz, yy, s = (z + z_step(q)) % NZ, (y + d % NY) % NY, q * NY + y
        return remote(
            sendb.at[yy, :, pl.ds(zz * CAP, CAP)], rx.at[:, x, pl.ds(s * CAP, CAP)],
            sem_a.at[s], at(zz, x, yy),
        )

    own = pltpu.make_async_copy(
        sendb.at[y, :, pl.ds(z * CAP, CAP)], rx.at[:, x, pl.ds(y * CAP, CAP)], sem_a.at[y]
    )
    own.start()

    @pl.loop(1, NS)
    def _(d):
        a_copy(d).start()

    for i in (0, 1):
        send(src_of(y2)[i], relays[i], rsem.at[i], via)
    for i, s in enumerate(src_of(yp)):
        send(s, dst_of(y, h)[i], wsem.at[y, i], dev_yp)
    for i, s in enumerate(src_of(ym)):
        send(s, dst_of(y, h)[i], wsem.at[y, i], dev_ym)

    def src_at(d):
        s = (d // NY) * NY + (y + NY - d % NY) % NY
        return s, pl.ds(s * CAP, CAP)

    def b_copies(d):
        s, r = src_at(d)
        blk = rx.at[:, x, r]
        return remote(blk, blk, sem_bp.at[s], dev_xp), remote(blk, blk, sem_bm.at[s], dev_xm)

    def c_copies(d):
        s, r = src_at(d)
        pb, mb = rx.at[0, xm, r], rx.at[1, xp, r]
        return remote(pb, pb, sem_cp.at[s], dev_xp), remote(mb, mb, sem_cm.at[s], dev_xm)

    def start_b(d):
        for cp in b_copies(d):
            cp.start()

    def start_c(d):
        s, r = src_at(d)
        arrived(rx.at[:, xm, r], sem_bp.at[s])
        arrived(rx.at[:, xp, r], sem_bm.at[s])
        for cp in c_copies(d):
            cp.start()

    def wait_a(d):
        s, r = src_at(d)
        arrived(rx.at[:, x, r], sem_a.at[s])

    own.wait()
    start_b(0)

    @pl.loop(1, LAG)
    def _(d):
        wait_a(d)
        start_b(d)

    @pl.loop(LAG, 8)
    def _(d):
        wait_a(d)
        start_b(d)
        start_c(d - LAG)

    arrived(relays[2], rsem.at[2])
    send(relays[2], dst_of(came, h)[2], wsem.at[came, 2], via)

    @pl.loop(8, 14)
    def _(d):
        wait_a(d)
        start_b(d)
        start_c(d - LAG)

    arrived(relays[0], rsem.at[0])
    send(relays[0], dst_of(came, h)[0], wsem.at[came, 0], via)

    @pl.loop(14, 20)
    def _(d):
        wait_a(d)
        start_b(d)
        start_c(d - LAG)

    arrived(relays[1], rsem.at[1])
    send(relays[1], dst_of(came, h)[1], wsem.at[came, 1], via)

    @pl.loop(20, NS)
    def _(d):
        wait_a(d)
        start_b(d)
        start_c(d - LAG)


    def swap(yy):
        for i in range(3):
            blk = dst_of(yy, h)[i]
            arrived(blk, wsem.at[yy, i])
            send(blk, blk, psem.at[yy, i], e, other)

    swap(yp)
    swap(ym)

    @pl.loop(NS - LAG, NS)
    def _(d):
        start_c(d)

    def unpack(b):
        @pl.loop(0, step // 16)
        def _(i):
            o = pl.multiple_of(b * step + i * 16, 16)
            for k in range(NX):
                r = pl.ds(pl.multiple_of(b * batch + k * step + i * 16, 16), 16)
                xr[r] = rx[0, k, pl.ds(o, 16)].reshape(16, wide)
                cr[r] = rx[1, k, pl.ds(o, 16)].reshape(16, wide)

    def wait_c(b):
        @pl.loop(b * (NS // NB), (b + 1) * (NS // NB))
        def _(d):
            s, r = src_at(d)
            arrived(rx.at[0, x2, r], sem_cp.at[s])
            arrived(rx.at[1, x2, r], sem_cm.at[s])

    wait_c(0)
    unpack(0)

    swap(y2)
    ho = pl.ds(pl.multiple_of(other * half, half), half)
    for cp in w_loads:
        cp.wait()
    for yy in (yp, ym, y2):
        for i in range(3):
            arrived(dst_of(yy, ho)[i], psem.at[yy, i])

    def chunk(k, b):
        return pl.ds(pl.multiple_of(b * batch + k * step, 16), step)

    class Scatter:
        def __init__(self, part, pos, dev_p, dev_m, b1p, b1m, b2p, b2m, sems):
            self.part, self.pos = part, pos
            self.devs, self.bufs, self.sems = (dev_p, dev_m), (b1p, b1m, b2p, b2m), sems
            self.kp, self.km, self.kf = (pos + 1) % 4, (pos + 3) % 4, (pos + 2) % 4
            w = part.shape[1]
            self.lo, self.hi = slice(0, w // 2), slice(w // 2, w)

        def start(self, b):
            r = slice(b * step, (b + 1) * step)
            b1p, b1m, b2p, b2m = self.bufs
            (p, m), lo, hi, sem = self.devs, self.lo, self.hi, self.sems
            far, kp, km = chunk(self.kf, b), chunk(self.kp, b), chunk(self.km, b)
            send(self.part.at[far, lo], b1p.at[r], sem.at[b, 0], p)
            send(self.part.at[far, hi], b1m.at[r], sem.at[b, 1], m)
            send(self.part.at[kp, hi], b2p.at[r, hi], sem.at[b, 2], p)
            send(self.part.at[km, lo], b2m.at[r, lo], sem.at[b, 3], m)

        def onward(self, b):
            r = slice(b * step, (b + 1) * step)
            b1p, b1m, b2p, b2m = self.bufs
            (p, m), lo, hi, sem = self.devs, self.lo, self.hi, self.sems
            for buf, k, cols, i, to, dev in (
                (b1p, self.kp, lo, 0, b2p, p), (b1m, self.km, hi, 1, b2m, m),
            ):
                arrived(buf.at[r], sem.at[b, i])
                c = chunk(k, b)
                self.part[c, cols] = (self.part[c, cols].astype(f32) + buf[r].astype(f32)).astype(bf16)
                send(self.part.at[c, cols], to.at[r, cols], sem.at[b, 4 + i], dev)

        def finish(self, b):
            r = slice(b * step, (b + 1) * step)
            _, _, b2p, b2m = self.bufs
            arrived(b2p.at[r, self.hi], self.sems.at[b, 2])
            arrived(b2m.at[r, self.lo], self.sems.at[b, 3])
            arrived(b2p.at[r, self.lo], self.sems.at[b, 4])
            arrived(b2m.at[r, self.hi], self.sems.at[b, 5])

    def forward(b):
        r = slice(b * batch, (b + 1) * batch)
        part[r, 0:ff] = jnp.dot(xr[r], wg[...], preferred_element_type=f32).astype(bf16)
        part[r, ff : 2 * ff] = jnp.dot(xr[r], wu[...], preferred_element_type=f32).astype(bf16)
        part[r, 2 * ff : 3 * ff] = lax.dot_general(
            cr[r], wd[...], NT, preferred_element_type=f32
        ).astype(bf16)

    def activate(b):
        @pl.loop(0, step // 16)
        def _(i):
            r = pl.ds(pl.multiple_of(b * step + i * 16, 16), 16)
            mr = pl.ds(pl.multiple_of(b * batch + y * step + i * 16, 16), 16)
            full = part[mr].astype(f32) + y2p[r].astype(f32) + y2m[r].astype(f32)
            g, u, pw = full[:, :ff], full[:, ff : 2 * ff], full[:, 2 * ff :]
            sig = jax.nn.sigmoid(g)
            act = g * sig
            hid = (act * u).astype(bf16)
            prod = hid.astype(f32) * pw
            lanes = prod[:, :128]
            for k in range(1, ff // 128):
                lanes = lanes + prod[:, k * 128 : (k + 1) * 128]
            mid[mr, 0:ff] = hid
            mid[mr, ff : 2 * ff] = (pw * u * sig * (1.0 + g * (1.0 - sig))).astype(bf16)
            mid[mr, 2 * ff : 3 * ff] = (pw * act).astype(bf16)
            top = lanes.astype(bf16)
            low = lanes - top.astype(f32)
            both = jnp.concatenate([top.astype(f32), low], axis=1).astype(bf16)
            dl[pl.ds(b * step + i * 16, 16)] = both.reshape(16, 2, 128)

    m_lo, m_hi = slice(0, 3 * ff // 2), slice(3 * ff // 2, 3 * ff)

    def block(k, b, cols):
        return mid.at[chunk(k, b), cols]

    def gather_start(b):
        for i, (cols, dev) in enumerate(((m_lo, dev_yp), (m_hi, dev_ym), (m_hi, dev_yp), (m_lo, dev_ym))):
            send(block(y, b, cols), block(y, b, cols), msem.at[b, i], dev)

    def gather_onward(b):
        arrived(block(ym, b, m_lo), msem.at[b, 0])
        send(block(ym, b, m_lo), block(ym, b, m_lo), msem.at[b, 4], dev_yp)
        arrived(block(yp, b, m_hi), msem.at[b, 1])
        send(block(yp, b, m_hi), block(yp, b, m_hi), msem.at[b, 5], dev_ym)

    def gather_finish(b):
        arrived(block(ym, b, m_hi), msem.at[b, 2])
        arrived(block(yp, b, m_lo), msem.at[b, 3])
        arrived(block(y2, b, m_lo), msem.at[b, 4])
        arrived(block(y2, b, m_hi), msem.at[b, 5])

    def backward(b):
        r = slice(b * batch, (b + 1) * batch)
        v = lax.dot_general(mid[r, ff : 2 * ff], wg[...], NT, preferred_element_type=f32)
        v = v + lax.dot_general(mid[r, 2 * ff : 3 * ff], wu[...], NT, preferred_element_type=f32)
        bk[r] = v.astype(bf16)

    def home(b):
        @pl.loop(0, step // 16)
        def _(i):
            o = pl.multiple_of(b * step + i * 16, 16)
            r = pl.ds(o, 16)
            mr = pl.ds(pl.multiple_of(b * batch + x * step + i * 16, 16), 16)
            full = bk[mr].astype(f32) + x2p[r].astype(f32) + x2m[r].astype(f32)
            retb[r, :, 0:half] = full.astype(bf16).reshape(16, 2, half)
            retb[r, :, half : half + 128] = dt[r]

        lo, hi = b * (NS // NB), (b + 1) * (NS // NB)

        @pl.loop(max(lo, 1), hi)
        def _(d):
            f_copy(d).start()

    def f_copy(d):
        s, r = src_at(d)
        return remote(
            retb.at[r], fin.at[y, pl.ds(z * CAP, CAP)], fsem.at[z * NY + y],
            at((z + NZ - z_step(d // NY)) % NZ, x, (y + NY - d % NY) % NY),
        )

    mine = pl.ds(pl.multiple_of(c * (ff // 2), ff // 2), ff // 2)
    theirs = pl.ds(pl.multiple_of(other * (ff // 2), ff // 2), ff // 2)
    to_core = y // 2
    o_cols = pl.ds(pl.multiple_of((y % 2) * wide, wide), wide)

    def out_copy(i):
        return remote(
            dout.at[pl.ds(i * ffd, ffd)], dg_hbm.at[0, :, o_cols], osem.at[y % 2],
            at(z, x, 2 * c + i), to_core,
        )

    def down_half(b):
        r = slice(b * batch, (b + 1) * batch)
        v = lax.dot_general(mid[r, 0:ff], cr[r], TN, preferred_element_type=f32)
        dd[...] = v if b == batches[0] else dd[...] + v

    fwd = Scatter(part, y, dev_yp, dev_ym, y1p, y1m, y2p, y2m, ysem)
    bwd = Scatter(bk, x, dev_xp, dev_xm, x1p, x1m, x2p, x2m, xsem)
    batches = tuple(range(NB))

    if STOP == 1:
        wait_c(1)
        unpack(1)
    if STOP > 1:
        forward(0)
        fwd.start(0)
        wait_c(1)
        unpack(1)
        forward(1)
        fwd.onward(0)
        fwd.start(1)
        fwd.onward(1)
        for b in batches:
            fwd.finish(b)
            activate(b)
            if STOP > 2:
                gather_start(b)

    if STOP > 2:
        dots_here = pltpu.make_async_copy(dl, dt, tsem.at[0])
        dots_there = remote(dl, dt, tsem.at[0], dev_t)

        @pl.when(x == y)
        def _():
            dots_here.start()

        @pl.when(x != y)
        def _():
            dots_there.start()

        first, last = batches[0], batches[-1]
        gather_onward(first)
        gather_finish(first)
        if STOP > 3:
            backward(first)
            bwd.start(first)
        gather_onward(last)
        if STOP > 3:
            down_half(first)
            bwd.onward(first)
        gather_finish(last)
        if STOP > 3:
            backward(last)
            bwd.start(last)
        arrived(dt, tsem.at[0])

    if STOP > 3:
        down_half(last)
        dsend[...] = dd[theirs].astype(bf16)
        send(dsend, drecv, dsem.at[0], e, other)
        bwd.onward(last)

    if STOP > 3:
        arrived(drecv, dsem.at[0])
        dout[...] = (dd[mine] + drecv[...].astype(f32)).astype(bf16)
        for i in range(2):
            here = (2 * c + i == y) & (to_core == c)

            @pl.when(here)
            def _():
                pltpu.make_async_copy(
                    dout.at[pl.ds(i * ffd, ffd)], dg_hbm.at[0, :, o_cols], osem.at[y % 2]
                ).start()

            @pl.when(jnp.logical_not(here))
            def _():
                out_copy(i).start()

    for b in batches:
        if STOP > 3:
            bwd.finish(b)
        if STOP > 4:
            home(b)

    if STOP > 4:
        back_own = pltpu.make_async_copy(
            retb.at[pl.ds(y * CAP, CAP)], fin.at[y, pl.ds(z * CAP, CAP)], fsem.at[z * NY + y]
        )
        back_own.start()
        back_own.wait()

        @pl.loop(1, NS)
        def _(d):
            zz, yy = (z + d // NY) % NZ, (y + d % NY) % NY
            arrived(fin.at[yy, pl.ds(zz * CAP, CAP)], fsem.at[zz * NY + yy])

        @pl.loop(1, NS)
        def _(d):
            f_copy(d).wait_send()

    for cp in sent:
        cp.wait_send()

    @pl.loop(1, NS)
    def _(d):
        a_copy(d).wait_send()

    @pl.loop(0, NS)
    def _(d):
        for cp in (*b_copies(d), *c_copies(d)):
            cp.wait_send()

    if STOP > 2:
        @pl.when(x != y)
        def _():
            dots_there.wait_send()

    if STOP > 3:
        for i in range(2):
            arrived(dg_hbm.at[0, :, i * wide : (i + 1) * wide], osem.at[i])

            @pl.when(jnp.logical_not((2 * c + i == y) & (to_core == c)))
            def _():
                out_copy(i).wait_send()


def exchange(logits, ids, tokens, cotangent, gate, up, down):
    tok_count, width = tokens.shape
    ffd = gate.shape[1]
    wide, ff, rows = width // NY, NY * ffd, NS * CAP
    half = wide // 2
    n = NX * rows
    vm = pltpu.VMEM
    dma = pltpu.SemaphoreType.DMA
    scratch = [
        vm((tok_count, width), bf16), vm((tok_count, width), bf16),
        vm((NY, 2, SLOTS, 2, half), bf16), vm((2, NX, rows, 2, half), bf16),
        vm((n, wide), bf16), vm((n, wide), bf16),
        vm((wide, ff), bf16), vm((wide, ff), bf16), vm((ff, wide), bf16),
        vm((half, ffd), bf16), vm((half, ffd), bf16), vm((ffd, half), bf16),
        vm((n, 3 * ff), bf16),
        vm((rows, 3 * ff // 2), bf16), vm((rows, 3 * ff // 2), bf16),
        vm((rows, 3 * ff), bf16), vm((rows, 3 * ff), bf16),
        vm((n, 3 * ff), bf16),
        vm((n, wide), bf16),
        vm((rows, half), bf16), vm((rows, half), bf16),
        vm((rows, wide), bf16), vm((rows, wide), bf16),
        vm((rows, 2, half + 128), bf16), vm((rows, 2, 128), bf16), vm((rows, 2, 128), bf16),
        vm((ff, wide), f32), vm((ff // 2, wide), bf16), vm((ff // 2, wide), bf16), vm((ff // 2, wide), bf16),
        dma((2,)), dma((3,)), dma((NS,)), dma((NS,)), dma((NS,)), dma((NS,)), dma((NS,)),
        dma((NY, 3)), dma((3,)), dma((NY, 3)),
        dma((NB, 6)), dma((NB, 6)), dma((NB, 6)), dma((NS,)), dma((1,)), dma((1,)), dma((2,)), dma((1,)),
    ]
    v, a = pl.BlockSpec(memory_space=pltpu.VMEM), pl.BlockSpec(memory_space=pl.ANY)
    return pl.pallas_call(
        kernel,
        out_shape=(
            jax.ShapeDtypeStruct(logits.shape, f32),
            jax.ShapeDtypeStruct((tok_count, 128), f32),
            jax.ShapeDtypeStruct((tok_count, 128), bf16),
            jax.ShapeDtypeStruct((NY, SLOTS, 2, half + 128), bf16),
            jax.ShapeDtypeStruct((1, ffd, width // 2), bf16),
        ),
        in_specs=[v, v, a, a, a, a, a],
        out_specs=(v, v, v, a, a),
        scratch_shapes=scratch,
        compiler_params=pltpu.CompilerParams(
            collective_id=0, has_side_effects=True, vmem_limit_bytes=62 * 1024 * 1024
        ),
        name="exchange",
    )(logits, ids, tokens, cotangent, gate, up, down)


def closing(named_ref, total_ref, take_ref, fin_ref, dg_in, tg_ref, lg_ref, dg_ref, acc):
    b = pl.program_id(0)
    half = fin_ref.shape[3] - 128
    dg_ref[...] = dg_in[...]
    v = fin_ref[0, :, :, 0:half].reshape(SLOTS, 2 * half)
    tg_ref[...] = jnp.dot(take_ref[:, :SLOTS], v, preferred_element_type=f32).astype(bf16)
    d = fin_ref[0, :, :, half : half + 128].reshape(SLOTS, 256).astype(f32)
    d = d[:, :128] + d[:, 128:]

    @pl.when(b == 0)
    def _():
        acc[...] = d

    @pl.when(b > 0)
    def _():
        acc[...] += d

    @pl.when(b == NY - 1)
    def _():
        dots = jnp.broadcast_to(jnp.sum(acc[...], axis=1, keepdims=True), (SLOTS, 128))
        top = dots.astype(bf16)
        low = (dots - top.astype(f32)).astype(bf16)
        slots = jnp.transpose(slot_map().astype(f32))[:SLOTS].astype(bf16)
        take = take_ref[:, :SLOTS]
        got = jnp.dot(take, slots * top, preferred_element_type=f32)
        got = got + jnp.dot(take, slots * low, preferred_element_type=f32)
        named, total = named_ref[...], total_ref[:, 0:1]
        held = named[:, :128]
        weight = weights_of(held, total).astype(f32)
        dweight = jnp.where(weight > 0.0, got / jnp.where(weight > 0.0, weight, 1.0), 0.0)
        inner = jnp.sum(dweight * held, axis=1, keepdims=True) / total
        rest = named[:, 128:]
        scale = SCALE / total
        lg_ref[:, :128] = scale * (dweight - inner) * held * (1.0 - held)
        lg_ref[:, 128:] = scale * (0.0 - inner) * rest * (1.0 - rest)


def per_device(tokens, cotangent, logits, expert_ids, gate_proj, up_proj, down_proj):
    tok_count, width = tokens.shape
    wide = width // NY
    ids = expert_ids.T
    ffd = gate_proj.shape[2]
    named, total, take, fin, dg = exchange(
        logits, ids, tokens, cotangent, gate_proj[0], up_proj[0], down_proj[0]
    )
    whole = lambda s: pl.BlockSpec(s, lambda b: (0,) * len(s))
    return pl.pallas_call(
        closing,
        grid=(NY,),
        out_shape=(
            jax.ShapeDtypeStruct(tokens.shape, bf16),
            jax.ShapeDtypeStruct(logits.shape, f32),
            jax.ShapeDtypeStruct(dg.shape, bf16),
        ),
        in_specs=[
            whole(named.shape), whole(total.shape), whole(take.shape),
            pl.BlockSpec((1,) + fin.shape[1:], lambda b: (b, 0, 0, 0)),
            pl.BlockSpec((1, ffd, wide // 2), lambda b: (0, 0, b)),
        ],
        out_specs=(
            pl.BlockSpec((tok_count, wide), lambda b: (0, b)),
            whole(logits.shape),
            pl.BlockSpec((1, ffd, wide // 2), lambda b: (0, 0, b)),
        ),
        scratch_shapes=[pltpu.VMEM((SLOTS, 128), f32)],
        name="closing",
    )(named, total, take, fin, dg)


def solution(mesh):
    rows = P(("expert", "dp"), None)
    mats = P("expert", None, None)
    return jax.shard_map(
        per_device,
        mesh=mesh,
        in_specs=(rows, rows, rows, rows, mats, mats, mats),
        out_specs=(rows, rows, P("expert", None, "dp")),
        check_vma=False,
    )
```

time: 165 us -> 141 us (0.85); the launches traced: 163 us -> 141 us
  other arithmetic: 7.09 us -> 0 us
  Pallas kernels: 148 us -> 141 us
  local copies, waits for them, and re-layouts: 6.76 us -> 0 us
    pallas_call x1 -> x2, Pallas kernels: 148 us -> 141 us  [the longest x1 136 us: exchange(): pl.pallas_call(kernel, out_shape=(jax.ShapeDtypeStruct(logits.shape, f32)...]
    reduce_sum x7 -> x0, other arithmetic: 4.76 us -> none  [the longest x1 2 us: per_device(): total = jnp.sum(chosen, axis=1, keepdims=True)]
    unnamed x7 -> x0, local copies, waits for them, and re-layouts: 4.65 us -> none
where the time goes in v2:
time: 141 us
  Pallas kernels  141 us (100%)
    pallas_call x1, Pallas kernels, exchange(): pl.pallas_call(kernel, out_shape=(jax.ShapeDtypeStruct(logits.shape, f32)...  136 us
    pallas_call x1, Pallas kernels, per_device(): pl.pallas_call(closing, grid=(NY,), out_shape=(jax.ShapeDtypeStruct(token...  4.99 us

profile of v2, /device:TPU:1, one launch (start us, length us, event | category | flops | bytes accessed | tf_op | source)
XLA Modules:
  0.0 141.2 jit_solution(7096286821350626492)
XLA Ops:
  0.6 135.5 %exchange.1 = (f32[128,256]{1,0:T(8,128)}, f32[128,128]{1,0:T(8,128)}, bf16[128,128]{1,0:T(8,128)(2,1)}, bf16[4,40,2,1024]{3,2,1,0:T(2,128)(2,1)}, bf16[1,128,3584]{2,1,0:T(8,128)(2,1)}) custom-call(f32[128,256]{1,0:T(8,128)} %logits_ref.1, s32[8,128]{1,0:T(8,128)} %bitcast.7, bf16[128,7168]{1,0:T(8,128)(2,1)} %tok_hbm.1, bf16[128,7168]{1,0:T(8,128)(2,1)} %cot_hbm.1, ...), custom_call_target="tpu_custom_call" | custom-call | tf_op jit(solution)/shard_map/exchange/pallas_call | solution.py:589
  136.2 5.0 %closing.1 = (bf16[128,7168]{1,0:T(8,128)(2,1)}, f32[128,256]{1,0:T(8,128)}, bf16[1,128,3584]{2,1,0:T(8,128)(2,1)}) custom-call(f32[128,256]{1,0:T(8,128)} %get-tuple-element.8.named_ref, f32[128,128]{1,0:T(8,128)} %get-tuple-element.9.total_ref, bf16[128,128]{1,0:T(8,128)(2,1)} %get-tuple-element.10.take_ref, ...), custom_call_target="tpu_custom_call" | custom-call | tf_op jit(solution)/shard_map/closing/pallas_call | solution.py:654

commit v3 on v2

--- a/solution.py
+++ b/solution.py
@@ -13,7 +13,6 @@
 PAD = 48
 LAG = 4
 NB = 2
-STOP = 99
 MESH = pl.DeviceIdType.MESH
 f32, bf16 = jnp.float32, jnp.bfloat16
 NT = (((1,), (1,)), ((), ()))
@@ -364,39 +363,45 @@
             lanes = prod[:, :128]
             for k in range(1, ff // 128):
                 lanes = lanes + prod[:, k * 128 : (k + 1) * 128]
-            mid[mr, 0:ff] = hid
-            mid[mr, ff : 2 * ff] = (pw * u * sig * (1.0 + g * (1.0 - sig))).astype(bf16)
-            mid[mr, 2 * ff : 3 * ff] = (pw * act).astype(bf16)
+            mid[mr, 2 * ff : 3 * ff] = hid
+            mid[mr, 0:ff] = (pw * u * sig * (1.0 + g * (1.0 - sig))).astype(bf16)
+            mid[mr, ff : 2 * ff] = (pw * act).astype(bf16)
             top = lanes.astype(bf16)
             low = lanes - top.astype(f32)
             both = jnp.concatenate([top.astype(f32), low], axis=1).astype(bf16)
             dl[pl.ds(b * step + i * 16, 16)] = both.reshape(16, 2, 128)
 
-    m_lo, m_hi = slice(0, 3 * ff // 2), slice(3 * ff // 2, 3 * ff)
+    gather_cols = (
+        (slice(0, ff), slice(ff, 2 * ff)),
+        (slice(2 * ff, 5 * ff // 2), slice(5 * ff // 2, 3 * ff)),
+    )
 
     def block(k, b, cols):
         return mid.at[chunk(k, b), cols]
 
-    def gather_start(b):
-        for i, (cols, dev) in enumerate(((m_lo, dev_yp), (m_hi, dev_ym), (m_hi, dev_yp), (m_lo, dev_ym))):
-            send(block(y, b, cols), block(y, b, cols), msem.at[b, i], dev)
-
-    def gather_onward(b):
-        arrived(block(ym, b, m_lo), msem.at[b, 0])
-        send(block(ym, b, m_lo), block(ym, b, m_lo), msem.at[b, 4], dev_yp)
-        arrived(block(yp, b, m_hi), msem.at[b, 1])
-        send(block(yp, b, m_hi), block(yp, b, m_hi), msem.at[b, 5], dev_ym)
-
-    def gather_finish(b):
-        arrived(block(ym, b, m_hi), msem.at[b, 2])
-        arrived(block(yp, b, m_lo), msem.at[b, 3])
-        arrived(block(y2, b, m_lo), msem.at[b, 4])
-        arrived(block(y2, b, m_hi), msem.at[b, 5])
+    def gather_start(b, g):
+        lo, hi = gather_cols[g]
+        for i, (cols, dev) in enumerate(((lo, dev_yp), (hi, dev_ym), (hi, dev_yp), (lo, dev_ym))):
+            send(block(y, b, cols), block(y, b, cols), msem.at[b, 6 * g + i], dev)
+
+    def gather_onward(b, g):
+        lo, hi = gather_cols[g]
+        arrived(block(ym, b, lo), msem.at[b, 6 * g])
+        send(block(ym, b, lo), block(ym, b, lo), msem.at[b, 6 * g + 4], dev_yp)
+        arrived(block(yp, b, hi), msem.at[b, 6 * g + 1])
+        send(block(yp, b, hi), block(yp, b, hi), msem.at[b, 6 * g + 5], dev_ym)
+
+    def gather_finish(b, g):
+        lo, hi = gather_cols[g]
+        arrived(block(ym, b, hi), msem.at[b, 6 * g + 2])
+        arrived(block(yp, b, lo), msem.at[b, 6 * g + 3])
+        arrived(block(y2, b, lo), msem.at[b, 6 * g + 4])
+        arrived(block(y2, b, hi), msem.at[b, 6 * g + 5])
 
     def backward(b):
         r = slice(b * batch, (b + 1) * batch)
-        v = lax.dot_general(mid[r, ff : 2 * ff], wg[...], NT, preferred_element_type=f32)
-        v = v + lax.dot_general(mid[r, 2 * ff : 3 * ff], wu[...], NT, preferred_element_type=f32)
+        v = lax.dot_general(mid[r, 0:ff], wg[...], NT, preferred_element_type=f32)
+        v = v + lax.dot_general(mid[r, ff : 2 * ff], wu[...], NT, preferred_element_type=f32)
         bk[r] = v.astype(bf16)
 
     def home(b):
@@ -435,102 +440,92 @@
 
     def down_half(b):
         r = slice(b * batch, (b + 1) * batch)
-        v = lax.dot_general(mid[r, 0:ff], cr[r], TN, preferred_element_type=f32)
+        v = lax.dot_general(mid[r, 2 * ff : 3 * ff], cr[r], TN, preferred_element_type=f32)
         dd[...] = v if b == batches[0] else dd[...] + v
 
     fwd = Scatter(part, y, dev_yp, dev_ym, y1p, y1m, y2p, y2m, ysem)
     bwd = Scatter(bk, x, dev_xp, dev_xm, x1p, x1m, x2p, x2m, xsem)
     batches = tuple(range(NB))
 
-    if STOP == 1:
-        wait_c(1)
-        unpack(1)
-    if STOP > 1:
-        forward(0)
-        fwd.start(0)
-        wait_c(1)
-        unpack(1)
-        forward(1)
-        fwd.onward(0)
-        fwd.start(1)
-        fwd.onward(1)
-        for b in batches:
-            fwd.finish(b)
-            activate(b)
-            if STOP > 2:
-                gather_start(b)
-
-    if STOP > 2:
-        dots_here = pltpu.make_async_copy(dl, dt, tsem.at[0])
-        dots_there = remote(dl, dt, tsem.at[0], dev_t)
-
-        @pl.when(x == y)
+    forward(0)
+    fwd.start(0)
+    wait_c(1)
+    unpack(1)
+    forward(1)
+    fwd.onward(0)
+    fwd.start(1)
+    fwd.onward(1)
+    for b in batches:
+        fwd.finish(b)
+        activate(b)
+        gather_start(b, 0)
+
+    dots_here = pltpu.make_async_copy(dl, dt, tsem.at[0])
+    dots_there = remote(dl, dt, tsem.at[0], dev_t)
+
+    @pl.when(x == y)
+    def _():
+        dots_here.start()
+
+    @pl.when(x != y)
+    def _():
+        dots_there.start()
+
+    gather_onward(0, 0)
+    gather_start(0, 1)
+    gather_onward(1, 0)
+    gather_start(1, 1)
+    gather_finish(0, 0)
+    backward(0)
+    bwd.start(0)
+    gather_onward(0, 1)
+    gather_finish(1, 0)
+    backward(1)
+    bwd.onward(0)
+    bwd.start(1)
+    gather_onward(1, 1)
+    gather_finish(0, 1)
+    down_half(0)
+    gather_finish(1, 1)
+    down_half(1)
+    dsend[...] = dd[theirs].astype(bf16)
+    send(dsend, drecv, dsem.at[0], e, other)
+    arrived(dt, tsem.at[0])
+    bwd.onward(1)
+    bwd.finish(0)
+    home(0)
+    arrived(drecv, dsem.at[0])
+    dout[...] = (dd[mine] + drecv[...].astype(f32)).astype(bf16)
+    for i in range(2):
+        here = (2 * c + i == y) & (to_core == c)
+
+        @pl.when(here)
         def _():
-            dots_here.start()
-
-        @pl.when(x != y)
+            pltpu.make_async_copy(
+                dout.at[pl.ds(i * ffd, ffd)], dg_hbm.at[0, :, o_cols], osem.at[y % 2]
+            ).start()
+
+        @pl.when(jnp.logical_not(here))
         def _():
-            dots_there.start()
-
-        first, last = batches[0], batches[-1]
-        gather_onward(first)
-        gather_finish(first)
-        if STOP > 3:
-            backward(first)
-            bwd.start(first)
-        gather_onward(last)
-        if STOP > 3:
-            down_half(first)
-            bwd.onward(first)
-        gather_finish(last)
-        if STOP > 3:
-            backward(last)
-            bwd.start(last)
-        arrived(dt, tsem.at[0])
-
-    if STOP > 3:
-        down_half(last)
-        dsend[...] = dd[theirs].astype(bf16)
-        send(dsend, drecv, dsem.at[0], e, other)
-        bwd.onward(last)
-
-    if STOP > 3:
-        arrived(drecv, dsem.at[0])
-        dout[...] = (dd[mine] + drecv[...].astype(f32)).astype(bf16)
-        for i in range(2):
-            here = (2 * c + i == y) & (to_core == c)
-
-            @pl.when(here)
-            def _():
-                pltpu.make_async_copy(
-                    dout.at[pl.ds(i * ffd, ffd)], dg_hbm.at[0, :, o_cols], osem.at[y % 2]
-                ).start()
-
-            @pl.when(jnp.logical_not(here))
-            def _():
-                out_copy(i).start()
-
-    for b in batches:
-        if STOP > 3:
-            bwd.finish(b)
-        if STOP > 4:
-            home(b)
-
-    if STOP > 4:
-        back_own = pltpu.make_async_copy(
-            retb.at[pl.ds(y * CAP, CAP)], fin.at[y, pl.ds(z * CAP, CAP)], fsem.at[z * NY + y]
-        )
-        back_own.start()
-        back_own.wait()
-
-        @pl.loop(1, NS)
-        def _(d):
-            zz, yy = (z + d // NY) % NZ, (y + d % NY) % NY
-            arrived(fin.at[yy, pl.ds(zz * CAP, CAP)], fsem.at[zz * NY + yy])
-
-        @pl.loop(1, NS)
-        def _(d):
-            f_copy(d).wait_send()
+            out_copy(i).start()
+
+    bwd.finish(1)
+    home(1)
+
+    back_own = pltpu.make_async_copy(
+        retb.at[pl.ds(y * CAP, CAP)], fin.at[y, pl.ds(z * CAP, CAP)], fsem.at[z * NY + y]
+    )
+    back_own.start()
+    back_own.wait()
+
+    @pl.loop(1, NS)
+    def _(d):
+        zz, yy = (z + d // NY) % NZ, (y + d % NY) % NY
+        arrived(fin.at[yy, pl.ds(zz * CAP, CAP)], fsem.at[zz * NY + yy])
+
+    @pl.loop(1, NS)
+    def _(d):
+        f_copy(d).wait_send()
 
     for cp in sent:
         cp.wait_send()
@@ -544,18 +539,16 @@
         for cp in (*b_copies(d), *c_copies(d)):
             cp.wait_send()
 
-    if STOP > 2:
-        @pl.when(x != y)
+    @pl.when(x != y)
+    def _():
+        dots_there.wait_send()
+
+    for i in range(2):
+        arrived(dg_hbm.at[0, :, i * wide : (i + 1) * wide], osem.at[i])
+
+        @pl.when(jnp.logical_not((2 * c + i == y) & (to_core == c)))
         def _():
-            dots_there.wait_send()
-
-    if STOP > 3:
-        for i in range(2):
-            arrived(dg_hbm.at[0, :, i * wide : (i + 1) * wide], osem.at[i])
-
-            @pl.when(jnp.logical_not((2 * c + i == y) & (to_core == c)))
-            def _():
-                out_copy(i).wait_send()
+            out_copy(i).wait_send()
 
 
 def exchange(logits, ids, tokens, cotangent, gate, up, down):
@@ -583,7 +576,7 @@
         vm((ff, wide), f32), vm((ff // 2, wide), bf16), vm((ff // 2, wide), bf16), vm((ff // 2, wide), bf16),
         dma((2,)), dma((3,)), dma((NS,)), dma((NS,)), dma((NS,)), dma((NS,)), dma((NS,)),
         dma((NY, 3)), dma((3,)), dma((NY, 3)),
-        dma((NB, 6)), dma((NB, 6)), dma((NB, 6)), dma((NS,)), dma((1,)), dma((1,)), dma((2,)), dma((1,)),
+        dma((NB, 6)), dma((NB, 12)), dma((NB, 6)), dma((NS,)), dma((1,)), dma((1,)), dma((2,)), dma((1,)),
     ]
     v, a = pl.BlockSpec(memory_space=pltpu.VMEM), pl.BlockSpec(memory_space=pl.ANY)
     return pl.pallas_call(

time: 141 us -> 139 us (0.986); the launches traced: 141 us -> 138 us
  Pallas kernels: 141 us -> 137 us
    pallas_call x1, Pallas kernels: 136 us -> 132 us  [exchange(): pl.pallas_call(kernel, out_shape=(jax.ShapeDtypeStruct(logits.shape, f32)...]
where the time goes in v3:
time: 139 us; the launch traced here: 138 us
  Pallas kernels  137 us (99%)
    pallas_call x1, Pallas kernels, exchange(): pl.pallas_call(kernel, out_shape=(jax.ShapeDtypeStruct(logits.shape, f32)...  132 us
    pallas_call x1, Pallas kernels, per_device(): pl.pallas_call(closing, grid=(NY,), out_shape=(jax.ShapeDtypeStruct(token...  4.98 us

profile of v3, /device:TPU:1, one launch (start us, length us, event | category | flops | bytes accessed | tf_op | source)
XLA Modules:
  0.0 137.7 jit_solution(17659222343193427493)
XLA Ops:
  0.6 132.0 %exchange.1 = (f32[128,256]{1,0:T(8,128)}, f32[128,128]{1,0:T(8,128)}, bf16[128,128]{1,0:T(8,128)(2,1)}, bf16[4,40,2,1024]{3,2,1,0:T(2,128)(2,1)}, bf16[1,128,3584]{2,1,0:T(8,128)(2,1)}) custom-call(f32[128,256]{1,0:T(8,128)} %logits_ref.1, s32[8,128]{1,0:T(8,128)} %bitcast.7, bf16[128,7168]{1,0:T(8,128)(2,1)} %tok_hbm.1, bf16[128,7168]{1,0:T(8,128)(2,1)} %cot_hbm.1, ...), custom_call_target="tpu_custom_call" | custom-call | tf_op jit(solution)/shard_map/exchange/pallas_call | solution.py:582
  132.7 5.0 %closing.1 = (bf16[128,7168]{1,0:T(8,128)(2,1)}, f32[128,256]{1,0:T(8,128)}, bf16[1,128,3584]{2,1,0:T(8,128)(2,1)}) custom-call(f32[128,256]{1,0:T(8,128)} %get-tuple-element.8.named_ref, f32[128,128]{1,0:T(8,128)} %get-tuple-element.9.total_ref, bf16[128,128]{1,0:T(8,128)(2,1)} %get-tuple-element.10.take_ref, ...), custom_call_target="tpu_custom_call" | custom-call | tf_op jit(solution)/shard_map/closing/pallas_call | solution.py:647

commit v4 on v3

--- a/solution.py
+++ b/solution.py
@@ -266,12 +266,13 @@
             arrived(blk, wsem.at[yy, i])
             send(blk, blk, psem.at[yy, i], e, other)
 
+    @pl.loop(NS - LAG, NS)
+    def _(d):
+        start_c(d)
+
     swap(yp)
     swap(ym)
 
-    @pl.loop(NS - LAG, NS)
-    def _(d):
-        start_c(d)
 
     def unpack(b):
         @pl.loop(0, step // 16)

time: 139 us -> 137 us (0.986)
  no operation moved by 1% of the time
where the time goes in v4:
time: 137 us
  Pallas kernels  136 us (99%)
    pallas_call x1, Pallas kernels, exchange(): pl.pallas_call(kernel, out_shape=(jax.ShapeDtypeStruct(logits.shape, f32)...  131 us
    pallas_call x1, Pallas kernels, per_device(): pl.pallas_call(closing, grid=(NY,), out_shape=(jax.ShapeDtypeStruct(token...  4.99 us

profile of v4, /device:TPU:1, one launch (start us, length us, event | category | flops | bytes accessed | tf_op | source)
XLA Modules:
  0.0 136.6 jit_solution(8647513699381990194)
XLA Ops:
  0.6 130.9 %exchange.1 = (f32[128,256]{1,0:T(8,128)}, f32[128,128]{1,0:T(8,128)}, bf16[128,128]{1,0:T(8,128)(2,1)}, bf16[4,40,2,1024]{3,2,1,0:T(2,128)(2,1)}, bf16[1,128,3584]{2,1,0:T(8,128)(2,1)}) custom-call(f32[128,256]{1,0:T(8,128)} %logits_ref.1, s32[8,128]{1,0:T(8,128)} %bitcast.7, bf16[128,7168]{1,0:T(8,128)(2,1)} %tok_hbm.1, bf16[128,7168]{1,0:T(8,128)(2,1)} %cot_hbm.1, ...), custom_call_target="tpu_custom_call" | custom-call | tf_op jit(solution)/shard_map/exchange/pallas_call | solution.py:583
  131.5 5.0 %closing.1 = (bf16[128,7168]{1,0:T(8,128)(2,1)}, f32[128,256]{1,0:T(8,128)}, bf16[1,128,3584]{2,1,0:T(8,128)(2,1)}) custom-call(f32[128,256]{1,0:T(8,128)} %get-tuple-element.8.named_ref, f32[128,128]{1,0:T(8,128)} %get-tuple-element.9.total_ref, bf16[128,128]{1,0:T(8,128)(2,1)} %get-tuple-element.10.take_ref, ...), custom_call_target="tpu_custom_call" | custom-call | tf_op jit(solution)/shard_map/closing/pallas_call | solution.py:648
